TPU v7x, 32 devices: a whole 2x2x4 slice. The times are simulated.
32 devices in a mesh: scenes: 2 (over x), rows: 16 (over z, y, core).
Axes of the slice: x: 2, y: 2, z: 4, core: 2. Of those that a mesh axis runs over, the one named last changes fastest.
Arguments:
- images: float32 [64, 128, 128], P(('scenes', 'rows')), parts along dimension 0, may hold values from -6 to 6
- conv_weight: float32 [3, 3, 128, 128], replicated, may hold values from -0.1875 to 0.1875
- lift_weight: float32 [320, 128], replicated, may hold values from -0.5 to 0.5
- vol_weight: float32 [3, 3, 3, 32, 40], replicated, may hold values from -0.1875 to 0.1875
Outputs:
- filtered: float32 [64, 32, 48, 128], P(('scenes', 'rows')), parts along dimension 0
There are 2 independent parts, one for each index of `scenes`. A program takes and returns all parts, laid end to end along the dimension named above; an argument that names none is the same for every part. Nothing has to cross between parts.
All inputs are finite; a program needn't handle non-finite values.
Results may differ from a plain program's by a relative error of at most 0.0001.
Values sent between devices are 32-bit elements; how exact they have to be, the bound alone decides.
A program may use at most 128 MiB of HBM per device.

v0:
```python
import jax
import jax.numpy as jnp
from jax import lax
from jax.experimental import pallas as pl
from jax.experimental.pallas import tpu as pltpu
from jax.sharding import PartitionSpec as P

DISP = 48
CHUNK = 4
STEP = 8
MESH = pl.DeviceIdType.MESH
f32, bf16 = jnp.float32, jnp.bfloat16


def split(x):
    hi = x.astype(bf16)
    return hi, (x - hi.astype(f32)).astype(bf16)


def dot(a, b):
    return jnp.dot(a, b, preferred_element_type=f32)


def dot3(stacked, rows, hi, lo):
    both = dot(stacked, hi)
    return both[:rows] + both[rows:] + dot(stacked[:rows], lo)


def taps(y, size, lane):
    cols = y.shape[1]
    before = jnp.where(lane >= 1, pltpu.roll(y[:size], 1, 1), 0.0)
    after = jnp.where(lane < cols - 1, pltpu.roll(y[2 * size :], cols - 1, 1), 0.0)
    return y[size : 2 * size] + before + after


def turned(x, by, is_right):
    cols = x.shape[-1]
    cut = by % cols
    return x if cut == 0 else pltpu.roll(x, jnp.where(is_right, cols - cut, cut), 1)


def place_of():
    position = lax.axis_index("rows")
    quarter = lax.axis_size("rows") // 4
    starts = (position == quarter) | (position == 3 * quarter)
    ends = (position == quarter - 1) | (position == 3 * quarter - 1)
    is_right = (position < quarter) | (position >= 3 * quarter)
    return starts, ends, is_right


def gather(
    images, cw_far, lw_far, vw_far, feat_a, feat_b, vol_2,
    before, after, there, there_before, there_after, vol_f, conv_2, lift_2,
    here, cw, lw, vw, send, recv, load,
):
    me, size = lax.axis_index("rows"), lax.axis_size("rows")
    up, down, partner = [lax.rem(me + by, size) for by in (1, size - 1, size // 2)]
    starts, ends, is_right = place_of()
    half = size // 2
    rows, cin, cols = images.shape
    halo = rows + 2
    feat = lw.shape[0]
    outc, groups = vw.shape[3:]
    per = feat // groups
    depth = halo * groups
    lane = lax.broadcasted_iota(jnp.int32, (1, cols), 1)

    to_first, to_last = me == half - 1, me == half
    from_first, from_last = me == 0, me == size - 1
    mated = to_first | to_last | from_first | from_last
    mate = jnp.where(to_first, 0, jnp.where(to_last, size - 1, jnp.where(from_first, half - 1, half)))

    fills = [(vw_far, vw), (cw_far, cw), (lw_far, lw), (images, here)]
    fills = [pltpu.make_async_copy(x, y, load.at[n]) for n, (x, y) in enumerate(fills)]
    for one in fills:
        one.start()

    barrier = pltpu.get_barrier_semaphore()

    @pl.when(mated)
    def _():
        pl.semaphore_signal(barrier, inc=1, device_id={"rows": mate}, device_id_type=MESH)

    for to in (up, down, partner):
        pl.semaphore_signal(barrier, inc=1, device_id={"rows": to}, device_id_type=MESH)
    @pl.when(mated)
    def _():
        pl.semaphore_wait(barrier, 4)

    @pl.when(jnp.logical_not(mated))
    def _():
        pl.semaphore_wait(barrier, 3)

    def copy(n, source, target, to, out=None):
        return pltpu.make_async_remote_copy(
            src_ref=source,
            dst_ref=target,
            send_sem=send.at[n if out is None else out],
            recv_sem=recv.at[n],
            device_id={"rows": to},
            device_id_type=MESH,
        )

    last, first = pl.ds(rows - 2, 2), pl.ds(0, 2)
    across = copy(0, images, there, partner)
    near = [copy(1, images.at[last], before, up), copy(2, images.at[first], after, down)]
    relays = [copy(3, there.at[last], there_before, up), copy(4, there.at[first], there_after, down)]
    direct = [
        copy(3, images.at[last], there_before, 0, 5),
        copy(4, images.at[first], there_after, size - 1, 6),
    ]
    across.start()

    @pl.when(to_first)
    def _():
        direct[0].start()

    @pl.when(to_last)
    def _():
        direct[1].start()

    for one in near:
        one.start()

    for one in fills:
        one.wait()

    vol_f[...] = jnp.zeros_like(vol_f)
    for dd in range(3):
        for dc in range(3):
            for r in range(rows):
                for dr in range(3):
                    top = (dc * rows + r) * outc
                    left = dd * depth + (r + dr) * groups
                    vol_f[top : top + outc, left : left + groups] = vw[dr, dd, dc] * (1.0 / per)
    m = 3 * rows * outc
    vol_2[:m], vol_2[m:] = split(vol_f[...])
    wide = jnp.concatenate([cw[dr].reshape(3 * cin, cin) for dr in range(3)], axis=1)
    conv_2[: 3 * cin], conv_2[3 * cin :] = split(wide)
    lift = jnp.concatenate([lw[pl.ds(k, groups, stride=per), :] for k in range(per)], axis=0)
    lift_2[:feat], lift_2[feat:] = split(lift)

    def features(above, middle, below, result, cut):
        parts = []
        for s in range(rows + 4):
            if s < 2:
                x = jnp.where(starts, 0.0, above[s])
            elif s < rows + 2:
                x = middle[s - 2]
            else:
                x = jnp.where(ends, 0.0, below[s - 2 - rows])
            parts.append(split(x))
        for r in range(0, halo, 2):
            pair = (r, min(r + 1, halo - 1))
            hi, lo = [
                jnp.concatenate(
                    [jnp.concatenate([parts[t + k][i] for k in range(3)], axis=0) for t in pair], axis=1
                )
                for i in range(2)
            ]
            y = dot3(conv_2[...], 3 * cin, hi, lo)
            hidden = []
            for n, t in enumerate(pair):
                h = jnp.maximum(taps(y[:, n * cols : (n + 1) * cols], cin, lane), 0.0)
                if cut and t == 0:
                    h = jnp.where(starts, 0.0, h)
                if cut and t == halo - 1:
                    h = jnp.where(ends, 0.0, h)
                hidden.append(h)
            f = dot3(lift_2[...], feat, *split(jnp.concatenate(hidden, axis=1)))
            for n, t in enumerate(pair):
                for k in range(per):
                    part = f[k * groups : (k + 1) * groups, n * cols : (n + 1) * cols]
                    result[k, t * groups : (t + 1) * groups, :] = part

    across.wait_recv()

    @pl.when(jnp.logical_not(from_last))
    def _():
        relays[0].start()

    @pl.when(jnp.logical_not(from_first))
    def _():
        relays[1].start()

    for one in near:
        one.wait_recv()
    features(before, here, after, feat_a.at[0], True)
    for b in range(1, STEP):
        for k in range(per):
            feat_a[b, k] = turned(feat_a[0, k], -b, is_right)
    for one in relays:
        one.wait_recv()
    features(there_before, there, there_after, feat_b, False)
    for one in (across, *near):
        one.wait_send()

    @pl.when(jnp.logical_not(from_last))
    def _():
        relays[0].wait_send()

    @pl.when(jnp.logical_not(from_first))
    def _():
        relays[1].wait_send()

    @pl.when(to_first)
    def _():
        direct[0].wait_send()

    @pl.when(to_last)
    def _():
        direct[1].wait_send()


def compute(feat_a, first_b, vol_2, out, feat_b, cost_hi, cost_lo):
    _, _, is_right = place_of()
    per, depth, cols = first_b.shape
    m, padded = vol_2.shape
    m = m // 2
    lane = lax.broadcasted_iota(jnp.int32, (1, cols), 1)

    for buf in (cost_hi, cost_lo):
        buf[:depth] = jnp.zeros((depth, cols), bf16)
        tail = buf.shape[0] - (DISP + 1) * depth
        buf[(DISP + 1) * depth :] = jnp.zeros((tail, cols), bf16)
    reach = jnp.where(is_right, cols - 1 - lane, lane)

    def correlate(disparities):
        for base in range(0, depth, 16):
            at = slice(base, base + 16)
            for d in disparities:
                step, b = divmod(d, STEP)
                total = None
                for k in range(per):
                    if b == 0 and step > 0:
                        feat_b[step, k, at, :] = turned(first_b[k, at, :], STEP * step, is_right)
                    right = feat_b[step, k, at, :] if step else first_b[k, at, :]
                    term = feat_a[b, k, at, :] * right
                    total = term if total is None else total + term
                hi, lo = split(jnp.where(reach >= d, turned(total, b, is_right), 0.0))
                place = (d + 1) * depth + base
                cost_hi[place : place + 16, :] = hi
                cost_lo[place : place + 16, :] = lo

    def filtered(d):
        first, second = d * depth, (d + 1) * depth
        hi, lo = [
            jnp.concatenate([buf[first : first + padded, :], buf[second : second + padded, :]], axis=1)
            for buf in (cost_hi, cost_lo)
        ]
        y = dot3(vol_2[...], m, hi, lo)
        for h in range(2):
            z = taps(y[:, h * cols : (h + 1) * cols], m // 3, lane)
            out[pl.ds(d + h, m // 3, stride=DISP), :] = z

    correlate(range(CHUNK + 2))
    for d in range(0, DISP, CHUNK):
        correlate(range(d + CHUNK + 2, min(d + 2 * CHUNK + 2, DISP)))
        for e in range(d, d + CHUNK, 2):
            filtered(e)


def on_device(images, conv_weight, lift_weight, vol_weight):
    rows, cin, cols = images.shape
    outc, groups = vol_weight.shape[3:]
    feat = lift_weight.shape[0]
    per = feat // groups
    depth = (rows + 2) * groups
    padded = -(-3 * depth // 256) * 256
    m = 3 * rows * outc
    length = DISP * depth + padded
    vmem = pl.BlockSpec(memory_space=pltpu.VMEM)
    edge = pltpu.VMEM((2, cin, cols), f32)
    first_a, first_b, vol_2 = pl.pallas_call(
        gather,
        out_shape=[
            jax.ShapeDtypeStruct((STEP, per, depth, cols), f32),
            jax.ShapeDtypeStruct((per, depth, cols), f32),
            jax.ShapeDtypeStruct((2 * m, padded), bf16),
        ],
        in_specs=[pl.BlockSpec(memory_space=pltpu.HBM)] * 4,
        out_specs=[vmem] * 3,
        scratch_shapes=[
            edge,
            edge,
            pltpu.VMEM((rows, cin, cols), f32),
            edge,
            edge,
            pltpu.VMEM((m, padded), f32),
            pltpu.VMEM((6 * cin, 3 * cin), bf16),
            pltpu.VMEM((2 * feat, cin), bf16),
            pltpu.VMEM(images.shape, f32),
            pltpu.VMEM(conv_weight.shape, f32),
            pltpu.VMEM(lift_weight.shape, f32),
            pltpu.VMEM(vol_weight.shape, f32),
            pltpu.SemaphoreType.DMA((7,)),
            pltpu.SemaphoreType.DMA((5,)),
            pltpu.SemaphoreType.DMA((4,)),
        ],
        compiler_params=pltpu.CompilerParams(
            vmem_limit_bytes=32 << 20, collective_id=0, has_side_effects=True
        ),
    )(images, conv_weight, lift_weight, vol_weight)
    flat = pl.pallas_call(
        compute,
        out_shape=jax.ShapeDtypeStruct((rows * outc * DISP, cols), f32),
        in_specs=[vmem] * 3,
        out_specs=vmem,
        scratch_shapes=[
            pltpu.VMEM((-(-DISP // STEP), per, depth, cols), f32),
            pltpu.VMEM((length, cols), bf16),
            pltpu.VMEM((length, cols), bf16),
        ],
        compiler_params=pltpu.CompilerParams(vmem_limit_bytes=32 << 20),
    )(first_a, first_b, vol_2)
    return flat.reshape(rows, outc, DISP, cols)


def solution(mesh):
    placed = (P(("scenes", "rows"), None, None), P(), P(), P())
    return jax.shard_map(
        on_device,
        mesh=mesh,
        in_specs=placed,
        out_specs=P(("scenes", "rows"), None, None, None),
        check_vma=False,
    )
```

profile of v0, /device:TPU:1, one launch (start us, length us, event | category | flops | bytes accessed | tf_op | source)
XLA Modules:
  0.0 30.2 jit_solution(15748937878911069756)
XLA Ops:
  0.0 0.0 copy-start
  0.0 1.1 %copy-done = f32[3,3,128,128]{3,2,1,0:T(8,128)S(1)} copy-done((f32[3,3,128,128]{3,2,1,0:T(8,128)S(1)}, f32[3,3,128,128]{3,2,1,0:T(8,128)}, u32[]{:S(2)}) %copy-start) | copy-done | bytes 589848
  1.1 0.0 copy-start.1
  1.1 1.0 %copy-done.1 = f32[3,3,3,32,40]{4,3,2,1,0:T(8,128)S(1)} copy-done((f32[3,3,3,32,40]{4,3,2,1,0:T(8,128)S(1)}, f32[3,3,3,32,40]{4,3,2,1,0:T(8,128)}, u32[]{:S(2)}) %copy-start.1) | copy-done | bytes 138264
  2.1 0.0 copy-start.2
  2.1 0.9 %copy-done.2 = f32[320,128]{1,0:T(8,128)S(1)} copy-done((f32[320,128]{1,0:T(8,128)S(1)}, f32[320,128]{1,0:T(8,128)}, u32[]{:S(2)}) %copy-start.2) | copy-done | bytes 163864
  3.0 0.0 copy-start.3
  3.0 0.9 %copy-done.3 = f32[2,128,128]{2,1,0:T(8,128)S(1)} copy-done((f32[2,128,128]{2,1,0:T(8,128)S(1)}, f32[2,128,128]{2,1,0:T(8,128)}, u32[]{:S(2)}) %copy-start.3) | copy-done | bytes 131096
  3.9 19.3 %shard_map.46 = (f32[8,8,160,128]{3,2,1,0:T(8,128)S(1)}, f32[8,160,128]{2,1,0:T(8,128)S(1)}, bf16[384,512]{1,0:T(8,128)(2,1)S(1)}) custom-call(f32[2,128,128]{2,1,0:T(8,128)S(1)} %copy-done.3, f32[3,3,128,128]{3,2,1,0:T(8,128)S(1)} %copy-done, f32[320,128]{1,0:T(8,128)S(1)} %copy-done.2, f32[3,3,3,32,40]{4,3,2,1,0:T(8,128)S(1)} %copy-done.1), custom_call_target="tpu_custom_call" | custom-call | tf_op jit(solution)/shard_map/pallas_call | solution.py:274
  23.2 6.9 %shard_map.47 = f32[3072,128]{1,0:T(8,128)} custom-call(f32[8,8,160,128]{3,2,1,0:T(8,128)S(1)} %get-tuple-element.8.feat_a, f32[8,160,128]{2,1,0:T(8,128)S(1)} %get-tuple-element.9.first_b, bf16[384,512]{1,0:T(8,128)(2,1)S(1)} %get-tuple-element.10.vol_2), custom_call_target="tpu_custom_call" | custom-call | tf_op jit(solution)/shard_map/pallas_call | solution.py:304
Async XLA Ops:
  0.0 1.1 %copy-start = (f32[3,3,128,128]{3,2,1,0:T(8,128)S(1)}, f32[3,3,128,128]{3,2,1,0:T(8,128)}, u32[]{:S(2)}) copy-start(f32[3,3,128,128]{3,2,1,0:T(8,128)} %cw_far.1) | copy-start | bytes 1769476
  1.1 1.0 %copy-start.1 = (f32[3,3,3,32,40]{4,3,2,1,0:T(8,128)S(1)}, f32[3,3,3,32,40]{4,3,2,1,0:T(8,128)}, u32[]{:S(2)}) copy-start(f32[3,3,3,32,40]{4,3,2,1,0:T(8,128)} %vw_far.1) | copy-start | bytes 414724
  2.1 0.9 %copy-start.2 = (f32[320,128]{1,0:T(8,128)S(1)}, f32[320,128]{1,0:T(8,128)}, u32[]{:S(2)}) copy-start(f32[320,128]{1,0:T(8,128)} %lw_far.1) | copy-start | bytes 491524
  3.0 0.9 %copy-start.3 = (f32[2,128,128]{2,1,0:T(8,128)S(1)}, f32[2,128,128]{2,1,0:T(8,128)}, u32[]{:S(2)}) copy-start(f32[2,128,128]{2,1,0:T(8,128)} %images.1) | copy-start | bytes 393220
where the time goes:
time: 30.4 us; the launch traced here: 30.2 us
  Pallas kernels  26.3 us (87%)
  local copies, waits for them, and re-layouts  3.9 us (13%)
    pallas_call x1, Pallas kernels, on_device(): pl.pallas_call(gather, out_shape=[jax.ShapeDtypeStruct((STEP, per, depth,...  19.3 us
    pallas_call x1, Pallas kernels, on_device(): pl.pallas_call(compute, out_shape=jax.ShapeDtypeStruct((rows * outc * DIS...  6.93 us
    unnamed x8, local copies, waits for them, and re-layouts  3.9 us

commit v1 on v0

--- a/solution.py
+++ b/solution.py
@@ -300,7 +300,7 @@
         compiler_params=pltpu.CompilerParams(
             vmem_limit_bytes=32 << 20, collective_id=0, has_side_effects=True
         ),
-    )(images, conv_weight, lift_weight, vol_weight)
+    )(*[pltpu.with_memory_space_constraint(x, pltpu.HBM) for x in (images, conv_weight, lift_weight, vol_weight)])
     flat = pl.pallas_call(
         compute,
         out_shape=jax.ShapeDtypeStruct((rows * outc * DISP, cols), f32),

time: 30.4 us -> 25.8 us (0.85)
  local copies, waits for them, and re-layouts: 3.9 us -> 0 us
  Pallas kernels: 26.3 us -> 25.7 us
    unnamed x8 -> x0, local copies, waits for them, and re-layouts: 3.9 us -> none
    pallas_call x1, Pallas kernels: 19.3 us -> 18.8 us  [on_device(): pl.pallas_call(gather, out_shape=[jax.ShapeDtypeStruct((STEP, per, depth,...]
where the time goes in v1:
time: 25.8 us; the launch traced here: 25.7 us
  Pallas kernels  25.7 us (100%)
    pallas_call x1, Pallas kernels, on_device(): pl.pallas_call(gather, out_shape=[jax.ShapeDtypeStruct((STEP, per, depth,...  18.8 us
    pallas_call x1, Pallas kernels, on_device(): pl.pallas_call(compute, out_shape=jax.ShapeDtypeStruct((rows * outc * DIS...  6.91 us

profile of v1, /device:TPU:1, one launch (start us, length us, event | category | flops | bytes accessed | tf_op | source)
XLA Modules:
  0.0 25.7 jit_solution(12082927323311604372)
XLA Ops:
  0.0 18.8 %shard_map.46 = (f32[8,8,160,128]{3,2,1,0:T(8,128)S(1)}, f32[8,160,128]{2,1,0:T(8,128)S(1)}, bf16[384,512]{1,0:T(8,128)(2,1)S(1)}) custom-call(f32[2,128,128]{2,1,0:T(8,128)} %images.1, f32[3,3,128,128]{3,2,1,0:T(8,128)} %cw_far.1, f32[320,128]{1,0:T(8,128)} %lw_far.1, f32[3,3,3,32,40]{4,3,2,1,0:T(8,128)} %vw_far.1), custom_call_target="tpu_custom_call" | custom-call | tf_op jit(solution)/shard_map/pallas_call | solution.py:274
  18.8 6.9 %shard_map.47 = f32[3072,128]{1,0:T(8,128)} custom-call(f32[8,8,160,128]{3,2,1,0:T(8,128)S(1)} %get-tuple-element.8.feat_a, f32[8,160,128]{2,1,0:T(8,128)S(1)} %get-tuple-element.9.first_b, bf16[384,512]{1,0:T(8,128)(2,1)S(1)} %get-tuple-element.10.vol_2), custom_call_target="tpu_custom_call" | custom-call | tf_op jit(solution)/shard_map/pallas_call | solution.py:304
